TPU v7x, 128 devices: a whole 4x4x4 slice. The times are simulated.
128 devices in a mesh: cuts: 2 (over x_hi), section: 4 (over y), dp: 16 (over z, x_lo, core).
Axes of the slice: x: 4 (x_hi: 2, x_lo: 2; x = x_hi * 2 + x_lo), y: 4, z: 4, core: 2. Of those that a mesh axis runs over, the one named last changes fastest.
Arguments:
- activations: bfloat16 [2, 4, 4096, 4096], P('cuts', 'section', 'dp'), may hold values from -6 to 6
- upstream_grad: bfloat16 [2, 4, 4096, 4096], P('cuts', 'section', 'dp'), may hold values from -6 to 6
- routes: int32 [2, 4, 4096, 4], P('cuts', 'section', 'dp'), may hold values from 0 to 15, as said below
- router_probs: float32 [2, 4, 4096, 4], P('cuts', 'section', 'dp'), may hold values from 0.2 to 1
- gate_weight: bfloat16 [4, 5376, 4096], P('section', 'dp'), may hold values from -0.09375 to 0.09375
- up_weight: bfloat16 [4, 5376, 4096], P('section', 'dp'), may hold values from -0.09375 to 0.09375
- down_weight: bfloat16 [4, 5376, 4096], P('section', 'dp'), may hold values from -0.078125 to 0.078125
Outputs:
- grad_gate: bfloat16 [4, 5376, 4096], P('section', 'dp')
- grad_up: bfloat16 [4, 5376, 4096], P('section', 'dp')
- grad_down: bfloat16 [4, 5376, 4096], P('section', 'dp')
- prev_grad: bfloat16 [2, 4, 4096, 4096], P('cuts', 'section', 'dp')
Inputs may be any that keep to these rules, and one draw needn't show every extreme that they name: `routes`: each token names 4 different experts. In every aligned block of 256 tokens of one replica and section, from 32 to 64 tokens name expert 0, and in every draw some block has exactly 64.
All inputs are finite; a program needn't handle non-finite values.
Results may differ from a plain program's by a relative error of at most 0.025.
Values may be sent and summed in bfloat16 or wider, within the bound.
No kernel may reach another device: no remote copies, remote signals or barrier semaphores. Data moves between devices by JAX's collectives and lax.ppermute only.
A program may use at most 192 MiB of HBM per device.

v0:
```python
import jax
import jax.numpy as jnp
from jax import lax
from jax.sharding import PartitionSpec as P

CAP = 64


def from_behind(block, axis, distance):
    devices = range(lax.axis_size(axis))
    route = [(i - distance, i) for i in devices if i - distance in devices]
    return lax.ppermute(block, axis, route)


def contract_last(left, right):
    return lax.dot_general(
        left, right, (((1,), (1,)), ((), ())), preferred_element_type=jnp.float32
    )


def contract_first(left, right):
    return lax.dot_general(
        left, right, (((0,), (0,)), ((), ())), preferred_element_type=jnp.float32
    )


def per_device(
    activations, upstream_grad, routes, router_probs, gate_weight, up_weight, down_weight
):
    local_acts = activations[0, 0]
    local_grads = upstream_grad[0, 0]
    expert_hits = routes[0, 0] == 0
    router_weight = jnp.sum(jnp.where(expert_hits, router_probs[0, 0], jnp.float32(0.0)), axis=1)
    is_routed = jnp.any(expert_hits, axis=1)
    row_index = jnp.cumsum(is_routed.astype(jnp.int32)) - 1
    wanted = jnp.arange(CAP, dtype=jnp.int32)
    picker = ((row_index[None, :] == wanted[:, None]) & is_routed[None, :]).astype(jnp.bfloat16)
    scaled = (router_weight[:, None] * local_grads.astype(jnp.float32)).astype(jnp.bfloat16)
    packed_acts = jnp.dot(picker, local_acts, preferred_element_type=jnp.float32).astype(
        jnp.bfloat16
    )
    packed_grads = jnp.dot(picker, scaled, preferred_element_type=jnp.float32).astype(jnp.bfloat16)
    rows_acts, rows_grads = (
        lax.all_gather(packed_acts, "dp", axis=0, tiled=True),
        lax.all_gather(packed_grads, "dp", axis=0, tiled=True),
    )
    gate_local = gate_weight[0]
    up_local = up_weight[0]
    down_local = down_weight[0]
    gate_pre = contract_last(rows_acts, gate_local)
    up_pre = contract_last(rows_acts, up_local)
    sig_gate = jax.nn.sigmoid(gate_pre)
    silu_gate = gate_pre * sig_gate
    hidden = (silu_gate * up_pre).astype(jnp.bfloat16)
    hidden_grad = contract_last(rows_grads, down_local)
    gate_grad = (hidden_grad * up_pre * sig_gate * (1.0 + gate_pre * (1.0 - sig_gate))).astype(
        jnp.bfloat16
    )
    up_grad = (hidden_grad * silu_gate).astype(jnp.bfloat16)
    down_part = contract_first(hidden, rows_grads)
    gate_part = contract_first(gate_grad, rows_acts)
    up_part = contract_first(up_grad, rows_acts)
    gate_total, up_total, down_total = (
        lax.psum(gate_part.astype(jnp.bfloat16), "cuts").astype(jnp.float32),
        lax.psum(up_part.astype(jnp.bfloat16), "cuts").astype(jnp.float32),
        lax.psum(down_part.astype(jnp.bfloat16), "cuts").astype(jnp.float32),
    )
    input_rows = lax.psum_scatter(
        (
            jnp.dot(gate_grad, gate_local, preferred_element_type=jnp.float32)
            + jnp.dot(up_grad, up_local, preferred_element_type=jnp.float32)
        ).astype(jnp.bfloat16),
        "dp",
        scatter_dimension=0,
        tiled=True,
    )
    token_grad = contract_first(picker, input_rows).astype(jnp.bfloat16)
    prev_grad = from_behind(token_grad[None, None], "section", -1)
    grad_gate = gate_total.astype(jnp.bfloat16)[None]
    grad_up = up_total.astype(jnp.bfloat16)[None]
    grad_down = down_total.astype(jnp.bfloat16)[None]
    return (grad_gate, grad_up, grad_down, prev_grad)


def solution(mesh):
    placed = (
        P("cuts", "section", "dp", None),
        P("cuts", "section", "dp", None),
        P("cuts", "section", "dp", None),
        P("cuts", "section", "dp", None),
        P("section", "dp", None),
        P("section", "dp", None),
        P("section", "dp", None),
    )
    return jax.shard_map(
        per_device,
        mesh=mesh,
        in_specs=placed,
        out_specs=(
            P("section", "dp", None),
            P("section", "dp", None),
            P("section", "dp", None),
            P("cuts", "section", "dp", None),
        ),
        check_vma=False,
    )
```

profile of v0, /device:TPU:1, one launch (start us, length us, event | category | flops | bytes accessed | tf_op | source)
XLA Modules:
  0.0 471.8 jit_solution(16867495214857487981)
XLA Ops:
  7.2 0.9 select_reduce_fusion
  8.7 2.9 convolution_convert_fusion.4
  11.7 3.0 convolution_convert_fusion.5
  14.8 52.8 %all-gather.5.cloned.1.call-done = bf16[1024,4096]{1,0:T(8,128)(2,1)} async-done(((bf16[64,4096]{1,0:T(8,128)(2,1)}), bf16[1024,4096]{1,0:T(8,128)(2,1)}) %all-gather.5.cloned.1.call-update) | async-done | bytes 8388624 | tf_op jit(solution)/shard_map/all_gather | solution.py:44
  67.6 7.6 %fusion.7 = f32[1024,336]{0,1:T(8,128)} fusion(bf16[1024,4096]{1,0:T(8,128)(2,1)} %all-gather.5.cloned.1.call-done, bf16[1,336,4096]{2,1,0:T(8,128)(2,1)S(1)} %copy-done), kind=kOutput, calls=%fused_computation.15 | convolution fusion | flops 2818572288 | bytes 12517376 | tf_op jit(solution)/shard_map/dot_general | solution.py:16
  75.2 4.1 fusion.10
  79.3 43.7 %all-gather.3.cloned.1.call-done = bf16[1024,4096]{1,0:T(8,128)(2,1)} async-done(((bf16[64,4096]{1,0:T(8,128)(2,1)}), bf16[1024,4096]{1,0:T(8,128)(2,1)}) %all-gather.3.cloned.1.call-update) | async-done | bytes 8388624 | tf_op jit(solution)/shard_map/all_gather | solution.py:45
  123.0 8.3 %multiply_convert_fusion.1 = (bf16[1024,336]{0,1:T(8,128)(2,1)S(1)}, bf16[1024,336]{0,1:T(8,128)(2,1)S(1)}) fusion(f32[1024,336]{0,1:T(8,128)} %fusion.7, f32[1024,336]{0,1:T(8,128)} %fusion.10, bf16[1024,4096]{1,0:T(8,128)(2,1)} %all-gather.3.cloned.1.call-done, bf16[1,336,4096]{2,1,0:T(8,128)(2,1)} %param.13), kind=kOutput, calls=%fused_computation.26 | convolution fusion | flops 2823045120 | bytes 15269888 | tf_op jit(solution)/shard_map/dot_general | solution.py:16
  131.4 8.3 %fusion.5 = f32[1024,4096]{1,0:T(8,128)} fusion(bf16[1024,336]{0,1:T(8,128)(2,1)S(1)} %get-tuple-element.10, bf16[1,336,4096]{2,1,0:T(8,128)(2,1)S(1)} %copy-done), kind=kOutput, calls=%fused_computation.13 | convolution fusion | flops 2818572288 | bytes 20217856 | tf_op jit(solution)/shard_map/dot_general | solution.py:70
  139.7 10.2 %add_convert_fusion = bf16[1024,4096]{1,0:T(8,128)(2,1)} fusion(f32[1024,4096]{1,0:T(8,128)} %fusion.5, bf16[1024,336]{0,1:T(8,128)(2,1)S(1)} %get-tuple-element.9, bf16[1,336,4096]{2,1,0:T(8,128)(2,1)S(1)} %copy-done.5), kind=kOutput, calls=%fused_computation | convolution fusion | flops 2826960896 | bytes 28606464 | tf_op jit(solution)/shard_map/dot_general | solution.py:71
  150.0 7.8 %fusion.1 = bf16[1,336,4096]{2,1,0:T(8,128)(2,1)} fusion(bf16[1024,336]{0,1:T(8,128)(2,1)S(1)} %get-tuple-element.9, bf16[1024,4096]{1,0:T(8,128)(2,1)} %all-gather.5.cloned.1.call-done), kind=kOutput, calls=%fused_computation.6 | convolution fusion | flops 2819948544 | bytes 11829248 | tf_op jit(solution)/shard_map/dot_general | solution.py:22
  157.8 8.2 %fusion = bf16[1,336,4096]{2,1,0:T(8,128)(2,1)} fusion(bf16[1024,336]{0,1:T(8,128)(2,1)S(1)} %copy-done.9, bf16[1024,4096]{1,0:T(8,128)(2,1)} %all-gather.5.cloned.1.call-done), kind=kOutput, calls=%fused_computation.5 | convolution fusion | flops 2819948544 | bytes 11829248 | tf_op jit(solution)/shard_map/dot_general | solution.py:22
  166.1 4.5 fusion.2
  170.6 76.1 %reduce-scatter.2.cloned.1.call-done = bf16[64,4096]{1,0:T(8,128)(2,1)} async-done(((bf16[1024,4096]{1,0:T(8,128)(2,1)}), bf16[64,4096]{1,0:T(8,128)(2,1)}) %reduce-scatter.2.cloned.1.call-update) | async-done | bytes 524304 | tf_op jit(solution)/shard_map/reduce_scatter | solution.py:68
  246.7 1.8 fusion.3
  248.5 1.3 collective-permute-start
  249.8 45.3 %collective-permute-done = bf16[1,1,256,4096]{3,2,1,0:T(8,128)(2,1)S(1)} collective-permute-done((bf16[1,1,256,4096]{3,2,1,0:T(8,128)(2,1)S(1)}, bf16[1,1,256,4096]{3,2,1,0:T(8,128)(2,1)S(1)}, u32[]{:S(2)}, u32[]{:S(2)}) %collective-permute-start) | collective-permute-done | bytes 2097184 | tf_op jit(solution)/shard_map/ppermute | solution.py:12
  295.0 159.8 %all-reduce.3.cloned.1.call-done = (bf16[1,336,4096]{2,1,0:T(8,128)(2,1)}, bf16[1,336,4096]{2,1,0:T(8,128)(2,1)}, bf16[1,336,4096]{2,1,0:T(8,128)(2,1)}) async-done(((bf16[1,336,4096]{2,1,0:T(8,128)(2,1)}, bf16[1,336,4096]{2,1,0:T(8,128)(2,1)}, bf16[1,336,4096]{2,1,0:T(8,128)(2,1)}), (bf16[1,336,4096]{2,1,0:T(8,128)(2,1)}, bf16[1,336,4096]{2,1,0:T(8,128)(2,1)}, ...) | async-done | bytes 8257552 | tf_op jit(solution)/shard_map/psum | solution.py:64
  454.8 3.8 copy.15
  458.6 1.5 copy.16
  460.1 1.2 copy-done.2
  461.4 1.5 copy.17
  462.9 1.0 copy-done.7
  463.9 1.3 copy.18
  (44 shorter events, 0.9 us)
Async XLA Ops:
  7.2 60.4 %copy-start = (bf16[1,336,4096]{2,1,0:T(8,128)(2,1)S(1)}, bf16[1,336,4096]{2,1,0:T(8,128)(2,1)}, u32[]{:S(2)}) copy-start(bf16[1,336,4096]{2,1,0:T(8,128)(2,1)} %param.11) | copy-start | bytes 8257540
  7.2 60.4 %all-gather.5.cloned.1.call-start = ((), (), s32[]{:S(2)}) async-start(), calls=%async_computation.2 | async-start | bytes 8912896 | tf_op jit(solution)/shard_map/all_gather | solution.py:44
  11.6 111.4 %all-gather.3.cloned.1.call-start = ((), (), s32[]{:S(2)}) async-start(), calls=%async_computation.1 | async-start | bytes 8912896 | tf_op jit(solution)/shard_map/all_gather | solution.py:45
  14.7 232.0 %reduce-scatter.2.cloned.1.call-start = ((), (), s32[]{:S(2)}) async-start(), calls=%async_computation.3 | async-start | bytes 8912896 | tf_op jit(solution)/shard_map/reduce_scatter | solution.py:68
  67.6 7.7 %copy-start.4 = (bf16[1,336,4096]{2,1,0:T(8,128)(2,1)S(1)}, bf16[1,336,4096]{2,1,0:T(8,128)(2,1)}, u32[]{:S(2)}) copy-start(bf16[1,336,4096]{2,1,0:T(8,128)(2,1)} %param.12) | copy-start | bytes 8257540
  67.6 7.7 %copy-start.10 = (bf16[1024,4096]{1,0:T(8,128)(2,1)S(1)}, bf16[1024,4096]{1,0:T(8,128)(2,1)}, u32[]{:S(2)}) copy-start(bf16[1024,4096]{1,0:T(8,128)(2,1)} %all-gather.5.cloned.1.call-done) | copy-start | bytes 25165828
  131.4 8.3 %copy-start.8 = (bf16[1024,336]{0,1:T(8,128)(2,1)}, bf16[1024,336]{0,1:T(8,128)(2,1)S(1)}, u32[]{:S(2)}) copy-start(bf16[1024,336]{0,1:T(8,128)(2,1)S(1)} %get-tuple-element.10) | copy-start | bytes 2064388
  131.4 8.3 %copy-start.5 = (bf16[1,336,4096]{2,1,0:T(8,128)(2,1)S(1)}, bf16[1,336,4096]{2,1,0:T(8,128)(2,1)}, u32[]{:S(2)}) copy-start(bf16[1,336,4096]{2,1,0:T(8,128)(2,1)} %param.12) | copy-start | bytes 8257540
  149.9 7.9 %copy-start.9 = (bf16[1024,336]{0,1:T(8,128)(2,1)S(1)}, bf16[1024,336]{0,1:T(8,128)(2,1)}, u32[]{:S(2)}) copy-start(bf16[1024,336]{0,1:T(8,128)(2,1)} %copy-done.8) | copy-start | bytes 2064388
  149.9 304.9 %all-reduce.3.cloned.1.call-start = ((), (), s32[]{:S(2)}) async-start(), calls=%async_computation.4 | async-start | bytes 16515072 | tf_op jit(solution)/shard_map/psum | solution.py:64
  150.0 16.1 %slice-start = ((s8[8388608]{0:T(1024)(128)(4,1)}), s8[4194304]{0:T(1024)(128)(4,1)S(1)}, s32[]{:S(2)}) async-start(s8[8388608]{0:T(1024)(128)(4,1)} %bitcast.47), calls=%async_computation.5 | async-start | bytes 8388608
  157.8 8.3 %slice-start.1 = ((s8[8388608]{0:T(1024)(128)(4,1)}), s8[4194304]{0:T(1024)(128)(4,1)S(1)}, s32[]{:S(2)}) async-start(s8[8388608]{0:T(1024)(128)(4,1)} %bitcast.47), calls=%async_computation.6 | async-start | bytes 8388608
  157.8 8.3 %copy-start.11 = (f32[1024,336]{0,1:T(8,128)S(1)}, f32[1024,336]{0,1:T(8,128)}, u32[]{:S(2)}) copy-start(f32[1024,336]{0,1:T(8,128)} %fusion.7) | copy-start | bytes 4128772
  157.8 8.3 %copy-start.12 = (f32[1024,336]{0,1:T(8,128)S(1)}, f32[1024,336]{0,1:T(8,128)}, u32[]{:S(2)}) copy-start(f32[1024,336]{0,1:T(8,128)} %fusion.10) | copy-start | bytes 4128772
  248.5 46.6 %collective-permute-start = (bf16[1,1,256,4096]{3,2,1,0:T(8,128)(2,1)S(1)}, bf16[1,1,256,4096]{3,2,1,0:T(8,128)(2,1)S(1)}, u32[]{:S(2)}, u32[]{:S(2)}) collective-permute-start(bf16[1,1,256,4096]{3,2,1,0:T(8,128)(2,1)S(1)} %fusion.3), channel_id=1, source_target_pairs={{16,0},{32,16},{48,32},{17,1},{33,17},{49,33},{18,2},{34,18},{50,3... | collective-permute-start | bytes 6291464 | tf_op jit(solution)/shard_map/ppermute | solution.py:12
  295.0 159.8 %copy-start.6 = (bf16[1,1,256,4096]{3,2,1,0:T(8,128)(2,1)}, bf16[1,1,256,4096]{3,2,1,0:T(8,128)(2,1)S(1)}, u32[]{:S(2)}) copy-start(bf16[1,1,256,4096]{3,2,1,0:T(8,128)(2,1)S(1)} %collective-permute-done) | copy-start | bytes 6291460
  454.8 3.8 copy-start.3
  458.6 2.8 copy-start.2
  461.4 2.6 copy-start.7
  461.4 3.9 copy-start.1
Sparse Core Ops, SparseCore 0:
  11.8 55.7 all-gather.4
  69.9 53.1 all-gather.2
  150.0 96.6 reduce-scatter.1
  250.0 204.7 all-reduce.2
where the time goes:
time: 472 us
  waiting for transfers between devices  378 us (80%)
  matrix products  66.8 us (14%)
  between operations  13.9 us (3%)
  local copies, waits for them, and re-layouts  10.7 us (2%)
    psum x1, waiting for transfers between devices, per_device(): lax.psum(gate_part.astype(jnp.bfloat16), 'cuts').astype(jnp.float32)  160 us
    reduce_scatter x1, waiting for transfers between devices, per_device(): lax.psum_scatter((jnp.dot(gate_grad, gate_local, preferred_element_type=j...  76.1 us
    all_gather x1, waiting for transfers between devices, per_device(): lax.all_gather(packed_acts, 'dp', axis=0, tiled=True)  52.8 us
    ppermute x1, waiting for transfers between devices, from_behind(): return lax.ppermute(block, axis, route)  45.3 us
    all_gather x1, waiting for transfers between devices, per_device(): lax.all_gather(packed_grads, 'dp', axis=0, tiled=True)  43.7 us
    dot_general x4, matrix products, contract_first(): lax.dot_general(left, right, (((0,), (0,)), ((), ())), preferred_element_...  22.4 us
    dot_general x3, matrix products, contract_last(): lax.dot_general(left, right, (((1,), (1,)), ((), ())), preferred_element_...  20.1 us
    unnamed x34, local copies, waits for them, and re-layouts  10.5 us
  transfers between devices with their start and end apart: 5, of which 5 were waited for; matrix products, arithmetic and copies ran while one was open for 8% of the time, Pallas kernels for 0%

commit v1 on v0

--- a/solution.py
+++ b/solution.py
@@ -4,6 +4,11 @@
 from jax.sharding import PartitionSpec as P
 
 CAP = 64
+
+
+def add_all(x, axis):
+    shards = lax.all_gather(x, axis)
+    return jnp.sum(shards, axis=0)
 
 
 def from_behind(block, axis, distance):
@@ -61,7 +66,7 @@
     gate_part = contract_first(gate_grad, rows_acts)
     up_part = contract_first(up_grad, rows_acts)
     gate_total, up_total, down_total = (
-        lax.psum(gate_part.astype(jnp.bfloat16), "cuts").astype(jnp.float32),
+        add_all(gate_part.astype(jnp.bfloat16), "cuts").astype(jnp.float32),
         lax.psum(up_part.astype(jnp.bfloat16), "cuts").astype(jnp.float32),
         lax.psum(down_part.astype(jnp.bfloat16), "cuts").astype(jnp.float32),
     )

time: 472 us -> 487 us (1.032)
  other arithmetic: 1.32 us -> 7.47 us
  waiting for transfers between devices: 378 us -> 383 us
    all_gather x0 -> x1, waiting for transfers between devices: none -> 73.7 us  [add_all(): shards = lax.all_gather(x, axis)]
    ppermute x1, waiting for transfers between devices: 45.3 us -> 0.01 us  [from_behind(): return lax.ppermute(block, axis, route)]
    psum x1, waiting for transfers between devices: 160 us -> 141 us  [per_device(): lax.psum(up_part.astype(jnp.bfloat16), 'cuts').astype(jnp.float32)]
    reduce_sum x0 -> x1, other arithmetic: none -> 6.15 us  [add_all(): return jnp.sum(shards, axis=0)]
    unnamed x34 -> x27, local copies, waits for them, and re-layouts: 10.5 us -> 8.74 us
  transfers between devices with their start and end apart: 5 -> 6, of which waited for: 5 -> 5; matrix products, arithmetic and copies ran while one was open for 8% -> 10% of each run, Pallas kernels for 0% -> 0%
where the time goes in v1:
time: 487 us; the launch traced here: 486 us
  waiting for transfers between devices  383 us (79%)
  matrix products  71.3 us (15%)
  between operations  13.9 us (3%)
  local copies, waits for them, and re-layouts  8.94 us (2%)
  other arithmetic  7.47 us (2%)
    psum x1, waiting for transfers between devices, per_device(): lax.psum(up_part.astype(jnp.bfloat16), 'cuts').astype(jnp.float32)  141 us
    all_gather x1, waiting for transfers between devices, add_all(): shards = lax.all_gather(x, axis)  73.7 us
    reduce_scatter x1, waiting for transfers between devices, per_device(): lax.psum_scatter((jnp.dot(gate_grad, gate_local, preferred_element_type=j...  72 us
    all_gather x1, waiting for transfers between devices, per_device(): lax.all_gather(packed_acts, 'dp', axis=0, tiled=True)  52.8 us
    all_gather x1, waiting for transfers between devices, per_device(): lax.all_gather(packed_grads, 'dp', axis=0, tiled=True)  43.7 us
    dot_general x4, matrix products, contract_first(): lax.dot_general(left, right, (((0,), (0,)), ((), ())), preferred_element_...  26.7 us
    dot_general x3, matrix products, contract_last(): lax.dot_general(left, right, (((1,), (1,)), ((), ())), preferred_element_...  20.1 us
    dot_general x1, matrix products, per_device(): jnp.dot(up_grad, up_local, preferred_element_type=jnp.float32)  10.3 us
  transfers between devices with their start and end apart: 6, of which 5 were waited for; matrix products, arithmetic and copies ran while one was open for 10% of the time, Pallas kernels for 0%

profile of v1, /device:TPU:1, one launch (start us, length us, event | category | flops | bytes accessed | tf_op | source)
XLA Modules:
  0.0 486.4 jit_solution(14040392700092671228)
XLA Ops:
  7.2 0.9 select_reduce_fusion
  8.7 2.9 convolution_convert_fusion.4
  11.7 3.0 convolution_convert_fusion.5
  14.8 52.8 %all-gather.7.cloned.1.call-done = bf16[1024,4096]{1,0:T(8,128)(2,1)} async-done(((bf16[64,4096]{1,0:T(8,128)(2,1)}), bf16[1024,4096]{1,0:T(8,128)(2,1)}) %all-gather.7.cloned.1.call-update) | async-done | bytes 8388624 | tf_op jit(solution)/shard_map/all_gather | solution.py:49
  67.6 7.6 %fusion.6 = f32[1024,336]{0,1:T(8,128)} fusion(bf16[1024,4096]{1,0:T(8,128)(2,1)} %all-gather.7.cloned.1.call-done, bf16[1,336,4096]{2,1,0:T(8,128)(2,1)S(1)} %copy-done), kind=kOutput, calls=%fused_computation.14 | convolution fusion | flops 2818572288 | bytes 12517376 | tf_op jit(solution)/shard_map/dot_general | solution.py:21
  75.2 4.1 fusion.9
  79.3 43.7 %all-gather.5.cloned.1.call-done = bf16[1024,4096]{1,0:T(8,128)(2,1)} async-done(((bf16[64,4096]{1,0:T(8,128)(2,1)}), bf16[1024,4096]{1,0:T(8,128)(2,1)}) %all-gather.5.cloned.1.call-update) | async-done | bytes 8388624 | tf_op jit(solution)/shard_map/all_gather | solution.py:50
  123.0 8.3 %multiply_convert_fusion.1 = (bf16[1024,336]{0,1:T(8,128)(2,1)S(1)}, bf16[1024,336]{0,1:T(8,128)(2,1)S(1)}) fusion(f32[1024,336]{0,1:T(8,128)} %fusion.6, f32[1024,336]{0,1:T(8,128)} %fusion.9, bf16[1024,4096]{1,0:T(8,128)(2,1)} %all-gather.5.cloned.1.call-done, bf16[1,336,4096]{2,1,0:T(8,128)(2,1)} %param.13), kind=kOutput, calls=%fused_computation.25 | convolution fusion | flops 2823045120 | bytes 15269888 | tf_op jit(solution)/shard_map/dot_general | solution.py:21
  131.4 8.4 %fusion.4 = f32[1024,4096]{1,0:T(8,128)} fusion(bf16[1024,336]{0,1:T(8,128)(2,1)S(1)} %get-tuple-element.9, bf16[1,336,4096]{2,1,0:T(8,128)(2,1)S(1)} %copy-done), kind=kOutput, calls=%fused_computation.12 | convolution fusion | flops 2818572288 | bytes 20217856 | tf_op jit(solution)/shard_map/dot_general | solution.py:75
  139.8 10.3 %add_convert_fusion = bf16[1024,4096]{1,0:T(8,128)(2,1)} fusion(f32[1024,4096]{1,0:T(8,128)} %fusion.4, bf16[1024,336]{0,1:T(8,128)(2,1)S(1)} %get-tuple-element.8, bf16[1,336,4096]{2,1,0:T(8,128)(2,1)S(1)} %copy-done.4), kind=kOutput, calls=%fused_computation | convolution fusion | flops 2826960896 | bytes 28606464 | tf_op jit(solution)/shard_map/dot_general | solution.py:76
  150.1 1.0 copy-done.8
  151.2 7.7 %convolution_convert_fusion.2 = bf16[336,4096]{1,0:T(8,128)(2,1)} fusion(bf16[1024,336]{0,1:T(8,128)(2,1)S(1)} %copy-done.8, bf16[1024,4096]{1,0:T(8,128)(2,1)} %all-gather.7.cloned.1.call-done), kind=kOutput, calls=%fused_computation.3 | convolution fusion | flops 2819948544 | bytes 11829248 | tf_op jit(solution)/shard_map/dot_general | solution.py:27
  158.9 8.1 %fusion = bf16[1,336,4096]{2,1,0:T(8,128)(2,1)} fusion(bf16[1024,336]{0,1:T(8,128)(2,1)S(1)} %get-tuple-element.8, bf16[1024,4096]{1,0:T(8,128)(2,1)} %all-gather.7.cloned.1.call-done), kind=kOutput, calls=%fused_computation.5 | convolution fusion | flops 2819948544 | bytes 11829248 | tf_op jit(solution)/shard_map/dot_general | solution.py:27
  167.0 7.8 %fusion.1 = bf16[1,336,4096]{2,1,0:T(8,128)(2,1)} fusion(bf16[1024,4096]{1,0:T(8,128)(2,1)} %all-gather.5.cloned.1.call-done, f32[1024,336]{0,1:T(8,128)S(1)} %copy-done.11, f32[1024,336]{0,1:T(8,128)S(1)} %copy-done.10), kind=kOutput, calls=%fused_computation.6 | convolution fusion | flops 2822012928 | bytes 13893632 | tf_op jit(solution)/shard_map/dot_general | solution.py:27
  174.9 72.0 %reduce-scatter.2.cloned.1.call-done = bf16[64,4096]{1,0:T(8,128)(2,1)} async-done(((bf16[1024,4096]{1,0:T(8,128)(2,1)}), bf16[64,4096]{1,0:T(8,128)(2,1)}) %reduce-scatter.2.cloned.1.call-update) | async-done | bytes 524304 | tf_op jit(solution)/shard_map/reduce_scatter | solution.py:73
  246.9 3.1 fusion.2
  250.0 1.3 collective-permute-start
  251.3 73.7 %all-gather.9.cloned.1.call-done = bf16[672,4096]{1,0:T(8,128)(2,1)} async-done(((bf16[336,4096]{1,0:T(8,128)(2,1)}), bf16[672,4096]{1,0:T(8,128)(2,1)}) %all-gather.9.cloned.1.call-update) | async-done | bytes 5505040 | tf_op jit(solution)/shard_map/all_gather | solution.py:10
  325.0 6.1 %reduce_sum.22 = bf16[336,4096]{1,0:T(8,128)(2,1)} reduce(bf16[2,336,4096]{2,1,0:T(8,128)(2,1)} %bitcast.47, bf16[]{:T(256)} %constant.15.clone.1), dimensions={0}, to_apply=%region_4.5 | reduce | flops 1376256 | bytes 8257538 | tf_op jit(solution)/shard_map/reduce_sum | solution.py:11
  331.2 141.0 %all-reduce.3.cloned.1.call-done = (bf16[1,336,4096]{2,1,0:T(8,128)(2,1)}, bf16[1,336,4096]{2,1,0:T(8,128)(2,1)}) async-done(((bf16[1,336,4096]{2,1,0:T(8,128)(2,1)}, bf16[1,336,4096]{2,1,0:T(8,128)(2,1)}), (bf16[1,336,4096]{2,1,0:T(8,128)(2,1)}, bf16[1,336,4096]{2,1,0:T(8,128)(2,1)})) %all-reduce.3.cloned.1.call-update) | async-done | bytes 5505040 | tf_op jit(solution)/shard_map/psum | solution.py:70
  472.2 3.8 copy.14
  476.0 1.5 copy.15
  477.5 1.0 copy-done.6
  478.6 1.3 copy.16
  (40 shorter events, 1.0 us)
Async XLA Ops:
  7.2 60.4 %copy-start = (bf16[1,336,4096]{2,1,0:T(8,128)(2,1)S(1)}, bf16[1,336,4096]{2,1,0:T(8,128)(2,1)}, u32[]{:S(2)}) copy-start(bf16[1,336,4096]{2,1,0:T(8,128)(2,1)} %param.11) | copy-start | bytes 8257540
  7.2 60.4 %all-gather.7.cloned.1.call-start = ((), (), s32[]{:S(2)}) async-start(), calls=%async_computation.2 | async-start | bytes 8912896 | tf_op jit(solution)/shard_map/all_gather | solution.py:49
  11.6 111.4 %all-gather.5.cloned.1.call-start = ((), (), s32[]{:S(2)}) async-start(), calls=%async_computation.1 | async-start | bytes 8912896 | tf_op jit(solution)/shard_map/all_gather | solution.py:50
  14.7 232.2 %reduce-scatter.2.cloned.1.call-start = ((), (), s32[]{:S(2)}) async-start(), calls=%async_computation.3 | async-start | bytes 8912896 | tf_op jit(solution)/shard_map/reduce_scatter | solution.py:73
  67.6 7.7 %copy-start.3 = (bf16[1,336,4096]{2,1,0:T(8,128)(2,1)S(1)}, bf16[1,336,4096]{2,1,0:T(8,128)(2,1)}, u32[]{:S(2)}) copy-start(bf16[1,336,4096]{2,1,0:T(8,128)(2,1)} %param.12) | copy-start | bytes 8257540
  67.6 7.7 %copy-start.9 = (bf16[1024,4096]{1,0:T(8,128)(2,1)S(1)}, bf16[1024,4096]{1,0:T(8,128)(2,1)}, u32[]{:S(2)}) copy-start(bf16[1024,4096]{1,0:T(8,128)(2,1)} %all-gather.7.cloned.1.call-done) | copy-start | bytes 25165828
  131.4 8.4 %copy-start.7 = (bf16[1024,336]{0,1:T(8,128)(2,1)}, bf16[1024,336]{0,1:T(8,128)(2,1)S(1)}, u32[]{:S(2)}) copy-start(bf16[1024,336]{0,1:T(8,128)(2,1)S(1)} %get-tuple-element.9) | copy-start | bytes 2064388
  131.4 8.4 %copy-start.4 = (bf16[1,336,4096]{2,1,0:T(8,128)(2,1)S(1)}, bf16[1,336,4096]{2,1,0:T(8,128)(2,1)}, u32[]{:S(2)}) copy-start(bf16[1,336,4096]{2,1,0:T(8,128)(2,1)} %param.12) | copy-start | bytes 8257540
  150.1 1.1 copy-start.8
  150.1 174.9 %all-gather.9.cloned.1.call-start = ((), (), s32[]{:S(2)}) async-start(), calls=%async_computation.4 | async-start | bytes 8257536 | tf_op jit(solution)/shard_map/all_gather | solution.py:10
  158.8 8.2 %copy-start.10 = (f32[1024,336]{0,1:T(8,128)S(1)}, f32[1024,336]{0,1:T(8,128)}, u32[]{:S(2)}) copy-start(f32[1024,336]{0,1:T(8,128)} %fusion.6) | copy-start | bytes 4128772
  158.9 8.2 %copy-start.11 = (f32[1024,336]{0,1:T(8,128)S(1)}, f32[1024,336]{0,1:T(8,128)}, u32[]{:S(2)}) copy-start(f32[1024,336]{0,1:T(8,128)} %fusion.9) | copy-start | bytes 4128772
  158.9 313.3 %all-reduce.3.cloned.1.call-start = ((), (), s32[]{:S(2)}) async-start(), calls=%async_computation.5 | async-start | bytes 11010048 | tf_op jit(solution)/shard_map/psum | solution.py:70
  250.0 81.2 %collective-permute-start = (bf16[1,1,256,4096]{3,2,1,0:T(8,128)(2,1)}, bf16[1,1,256,4096]{3,2,1,0:T(8,128)(2,1)S(1)}, u32[]{:S(2)}, u32[]{:S(2)}) collective-permute-start(bf16[1,1,256,4096]{3,2,1,0:T(8,128)(2,1)} %fusion.2), channel_id=1, source_target_pairs={{16,0},{32,16},{48,32},{17,1},{33,17},{49,33},{18,2},{34,18},{50,3... | collective-permute-start | bytes 6291464 | tf_op jit(solution)/shard_map/ppermute | solution.py:17
  331.2 141.0 %copy-start.5 = (bf16[1,1,256,4096]{3,2,1,0:T(8,128)(2,1)}, bf16[1,1,256,4096]{3,2,1,0:T(8,128)(2,1)S(1)}, u32[]{:S(2)}) copy-start(bf16[1,1,256,4096]{3,2,1,0:T(8,128)(2,1)S(1)} %collective-permute-done) | copy-start | bytes 6291460
  472.2 3.8 copy-start.2
  476.0 2.6 copy-start.6
  476.0 3.9 copy-start.1
Sparse Core Ops, SparseCore 0:
  11.8 55.7 all-gather.6
  69.9 53.1 all-gather.4
  150.2 96.6 reduce-scatter.1
  249.0 75.9 all-gather.8
  328.1 144.0 all-reduce.2
